TPU v7x, 32 devices: a whole 2x2x4 slice. The times are simulated.
32 devices in a mesh: seq: 8 (over y, x, core), dp: 4 (over z).
Axes of the slice: x: 2, y: 2, z: 4, core: 2. Of those that a mesh axis runs over, the one named last changes fastest.
Arguments:
- tokens: bfloat16 [16384, 1024], P(('dp', 'seq')), parts along dimension 0, may hold values from -6 to 6
- norm_gain: float32 [1024], replicated, may hold values from 0.25 to 1.75
- query_weight: bfloat16 [1024, 1024], replicated
- key_weight: bfloat16 [1024, 1024], replicated
- value_weight: bfloat16 [1024, 1024], replicated, may hold values from -0.1875 to 0.1875
- out_weight: bfloat16 [1024, 1024], replicated, may hold values from -0.1875 to 0.1875
- random_blocks: int32 [256, 3], P('dp'), parts along dimension 0, may hold values from 0 to 63, as said below
- bucket_id: int32 [1], replicated, may hold values from 0 to 7
- global_positions: int32 [8, 128], replicated, may hold values from 0 to 4095, as said below
Outputs:
- layer_out: bfloat16 [16384, 1024], P(('dp', 'seq')), parts along dimension 0
There are 4 independent parts, one for each index of `dp`. A program takes and returns all parts, laid end to end along the dimension named above; an argument that names none is the same for every part. Nothing has to cross between parts.
Inputs may be any that keep to these rules, and one draw needn't show every extreme that they name: `random_blocks`: each row lists 3 block numbers. For the query blocks of one device (aligned runs of 8 rows) at most 3 of the listed blocks lie within the tokens of any one device, and exactly 3 for some device. A block may be listed more than once. `global_positions`: each row holds 128 distinct positions in rising order.
All inputs are finite; a program needn't handle non-finite values.
Results may differ from a plain program's by a relative error of at most 0.0089.
Values may be sent and summed in bfloat16 or wider, within the bound.
No kernel may reach another device: no remote copies, remote signals or barrier semaphores. Data moves between devices by JAX's collectives and lax.ppermute only.
A program may use at most 128 MiB of HBM per device.

v0:
```python
import jax
import jax.numpy as jnp
from jax import lax
from jax.sharding import PartitionSpec as P

HEADS = 16
HDIM = 64
BLOCK = 64
RAND = 3
NGLOB = 128


def with_halo(block, sides, width):
    for axis, dim in sides:
        count = lax.axis_size(axis)
        forward = [(i, i + 1) for i in range(count - 1)]
        forward.append((count - 1, 0))
        backward = [(target, source) for source, target in forward]
        low = lax.ppermute(
            lax.slice_in_dim(block, block.shape[dim] - width, None, axis=dim), axis, forward
        )
        high = lax.ppermute(lax.slice_in_dim(block, 0, width, axis=dim), axis, backward)
        block = jnp.concatenate([low, block, high], axis=dim)
    return block


def combined_all(value, axis, join):
    pieces = jax.tree.map(lambda part: lax.all_gather(part, axis), value)
    head = jax.tree.map(lambda part: part[0], pieces)
    tail = jax.tree.map(lambda part: part[1:], pieces)
    running, _ = lax.scan(lambda running, piece: (join(running, piece), None), head, tail)
    return running


def layer_norm(tokens, norm_gain):
    values = tokens.astype(jnp.float32)
    center = values - jnp.mean(values, axis=-1, keepdims=True)
    spread = jnp.mean(center * center, axis=-1, keepdims=True)
    return (center * lax.rsqrt(spread + 1e-05) * norm_gain).astype(jnp.bfloat16)


def combine_rows(first, second):
    top_score = jnp.maximum(first[0], second[0])
    first_factor = jnp.exp(first[0] - top_score)
    second_factor = jnp.exp(second[0] - top_score)
    total = first[1] * first_factor + second[1] * second_factor
    weighted = first[2] * first_factor[..., None] + second[2] * second_factor[..., None]
    return (top_score, total, weighted)


def body(
    tokens,
    norm_gain,
    query_weight,
    key_weight,
    value_weight,
    out_weight,
    random_blocks,
    bucket_id,
    global_positions,
):
    shards = lax.axis_size("seq")
    device = lax.axis_index("seq")
    rows_here = tokens.shape[0]
    width = tokens.shape[1]
    local_blocks = rows_here // BLOCK
    slots = local_blocks * RAND
    capacity = (slots + shards - 1) // shards
    scale = HDIM ** (-0.5)
    normed = layer_norm(tokens, norm_gain)
    queries = jnp.dot(normed, query_weight, preferred_element_type=jnp.float32).astype(jnp.bfloat16)
    key_rows = jnp.dot(normed, key_weight, preferred_element_type=jnp.float32).astype(jnp.bfloat16)
    value_rows = jnp.dot(normed, value_weight, preferred_element_type=jnp.float32).astype(
        jnp.bfloat16
    )
    paired = jnp.concatenate([key_rows, value_rows], axis=1)
    widened = with_halo(paired, (("seq", 0),), BLOCK)
    wide_blocks = widened.reshape(local_blocks + 2, BLOCK, 2 * width)
    window = jnp.stack([wide_blocks[:-2], wide_blocks[1:-1], wide_blocks[2:]], axis=1)
    window = window.reshape(local_blocks, 3 * BLOCK, 2 * width)
    table = random_blocks.reshape(shards, slots)
    my_table = lax.dynamic_slice_in_dim(table, device, 1, 0)[0]
    source = table // local_blocks
    inner = table % local_blocks
    match = (source == device).astype(jnp.int32)
    rank = jnp.cumsum(match, axis=1) - 1
    slot_iota = jnp.arange(capacity, dtype=jnp.int32)
    select = (match[:, :, None] == 1) & (rank[:, :, None] == slot_iota[None, None, :])
    send_index = jnp.sum(jnp.where(select, inner[:, :, None], 0), axis=1)
    blocks_here = paired.reshape(local_blocks, BLOCK, 2 * width)
    outgoing = blocks_here[send_index]
    incoming = lax.all_to_all(outgoing, "seq", split_axis=0, concat_axis=0, tiled=True)
    incoming = incoming.reshape(shards * capacity, BLOCK, 2 * width)
    my_source = my_table // local_blocks
    slot_order = jnp.arange(slots, dtype=jnp.int32)
    same = (my_source[:, None] == my_source[None, :]) & (slot_order[None, :] < slot_order[:, None])
    my_rank = jnp.sum(same.astype(jnp.int32), axis=1)
    random_rows = incoming[my_source * capacity + my_rank]
    random_rows = random_rows.reshape(local_blocks, RAND * BLOCK, 2 * width)
    positions = global_positions[bucket_id[0]]
    local_position = positions - device * rows_here
    selector = (local_position[:, None] == jnp.arange(rows_here, dtype=jnp.int32)[None, :]).astype(
        jnp.bfloat16
    )
    global_normed = lax.psum(
        jnp.dot(selector, normed, preferred_element_type=jnp.float32).astype(jnp.bfloat16), "seq"
    )
    global_queries = jnp.dot(
        global_normed, query_weight, preferred_element_type=jnp.float32
    ).astype(jnp.bfloat16)
    global_keys = jnp.dot(global_normed, key_weight, preferred_element_type=jnp.float32).astype(
        jnp.bfloat16
    )
    global_values = jnp.dot(global_normed, value_weight, preferred_element_type=jnp.float32).astype(
        jnp.bfloat16
    )
    global_paired = jnp.concatenate([global_keys, global_values], axis=1)
    global_broad = jnp.broadcast_to(global_paired[None], (local_blocks, NGLOB, 2 * width))
    key_set = jnp.concatenate([window, random_rows, global_broad], axis=1)
    count = key_set.shape[1]
    key_part = key_set[:, :, :width].reshape(local_blocks, count, HEADS, HDIM)
    value_part = key_set[:, :, width:].reshape(local_blocks, count, HEADS, HDIM)
    query_blocks = queries.reshape(local_blocks, BLOCK, HEADS, HDIM)
    scores = (
        jnp.einsum("bqhd,bkhd->bhqk", query_blocks, key_part, preferred_element_type=jnp.float32)
        * scale
    )
    top_score = jnp.max(scores, axis=-1, keepdims=True)
    expo = jnp.exp(scores - top_score)
    probs = (expo / jnp.sum(expo, axis=-1, keepdims=True)).astype(jnp.bfloat16)
    sparse_out = jnp.einsum(
        "bhqk,bkhd->bqhd", probs, value_part, preferred_element_type=jnp.float32
    )
    sparse_out = sparse_out.reshape(rows_here, width).astype(jnp.bfloat16)
    global_heads = global_queries.reshape(NGLOB, HEADS, HDIM)
    local_keys = key_rows.reshape(rows_here, HEADS, HDIM)
    local_values = value_rows.astype(jnp.float32).reshape(rows_here, HEADS, HDIM)
    global_scores = (
        jnp.einsum("qhd,khd->hqk", global_heads, local_keys, preferred_element_type=jnp.float32)
        * scale
    )
    global_top = jnp.max(global_scores, axis=-1)
    global_expo = jnp.exp(global_scores - global_top[..., None])
    global_total = jnp.sum(global_expo, axis=-1)
    global_weighted = jnp.einsum(
        "hqk,khd->hqd", global_expo, local_values, precision=lax.Precision.HIGHEST
    )
    merged = combined_all((global_top, global_total, global_weighted), "seq", combine_rows)
    global_out = merged[2] / merged[1][..., None]
    global_out = jnp.transpose(global_out, (1, 0, 2)).reshape(NGLOB, width).astype(jnp.bfloat16)
    placed = jnp.dot(selector.T, global_out, preferred_element_type=jnp.float32).astype(
        jnp.bfloat16
    )
    owned_row = jnp.sum(selector.astype(jnp.float32), axis=0) > 0.5
    mixed = jnp.where(owned_row[:, None], placed, sparse_out)
    return jnp.dot(mixed, out_weight, preferred_element_type=jnp.float32).astype(jnp.bfloat16)


def solution(mesh):
    placed = (P(("dp", "seq"), None), P(), P(), P(), P(), P(), P("dp", None), P(), P())
    return jax.shard_map(
        body, mesh=mesh, in_specs=placed, out_specs=P(("dp", "seq"), None), check_vma=False
    )
```

profile of v0, /device:TPU:0, one launch (start us, length us, event | category | flops | bytes accessed | tf_op | source)
XLA Modules:
  0.0 269.2 jit_solution(3711062153873412040)
XLA Ops:
  6.5 1.6 convert_reduce_fusion
  8.1 1.6 fusion.15
  9.8 3.1 %convolution_convert_fusion.4 = bf16[512,1024]{1,0:T(8,128)(2,1)S(1)} fusion(bf16[1024,1024]{1,0:T(8,128)(2,1)} %param.14, bf16[512,1024]{1,0:T(8,128)(2,1)S(1)} %copy-done.7, f32[1024]{0:T(1024)S(1)} %copy-done.16, f32[512]{0:T(512)S(1)} %add_rsqrt_fusion, f32[512]{0:T(512)S(1)} %broadcast_multiply_fusion), kind=kOutput, calls=%fused_computation.51 | convolution fusion | flops 1076887552 | bytes 4202496 | tf_op jit(solution)/shard_map/dot_general | solution.py:72
  12.9 1.3 convolution_convert_fusion.3
  14.3 0.8 fusion.29
  15.1 0.4 collective-permute-start
  15.6 2.9 %collective-permute-start.1 = (bf16[64,2048]{1,0:T(8,128)(2,1)}, bf16[64,2048]{1,0:T(8,128)(2,1)}, u32[]{:S(2)}, u32[]{:S(2)}) collective-permute-start(bf16[64,2048]{1,0:T(8,128)(2,1)} %get-tuple-element.99), channel_id=1, source_target_pairs={{4,0},{8,4},{12,8},{16,12},{20,16},{24,20},{28,24},{0,28},{5,1},{9... | collective-permute-start | bytes 786440 | tf_op jit(solution)/shard_map/ppermute | solution.py:22
  19.2 3.7 %collective-permute-done = bf16[64,2048]{1,0:T(8,128)(2,1)S(1)} collective-permute-done((bf16[64,2048]{1,0:T(8,128)(2,1)}, bf16[64,2048]{1,0:T(8,128)(2,1)S(1)}, u32[]{:S(2)}, u32[]{:S(2)}) %collective-permute-start) | collective-permute-done | bytes 262176 | tf_op jit(solution)/shard_map/ppermute | solution.py:19
  22.8 1.6 collective-permute-done.1
  24.5 6.7 %pad_maximum_fusion.5 = (bf16[512,2048]{1,0:T(8,128)(2,1)}, bf16[512,2048]{1,0:T(8,128)(2,1)}, bf16[512,2048]{1,0:T(8,128)(2,1)}) fusion(bf16[64,2048]{1,0:T(8,128)(2,1)S(1)} %collective-permute-done, bf16[512,1024]{1,0:T(8,128)(2,1)S(1)} %convolution_convert_fusion.3, bf16[512,1024]{1,0:T(8,128)(2,1)} %copy-done.3, bf16[64,2048]{1,0:T(8,128)(2,1)} %collective-permute-done.1), kind=kLoop, calls=%fused_computation.39 | loop fusion | flops 16777216 | bytes 8912896 | tf_op jit(solution)/shard_map/concatenate | solution.py:23
  31.2 6.0 %gather_fusion = bf16[24,64,2048]{2,1,0:T(8,128)(2,1)} fusion(bf16[8,64,2048]{2,1,0:T(8,128)(2,1)} %bitcast.101, s32[1024]{0:T(1024)S(1)} %pad_clamp_fusion.1), kind=kCustom, calls=%fused_computation | custom fusion | bytes 12583008 | tf_op jit(solution)/shard_map/gather | solution.py:91
  37.2 4.7 %all-to-all-start = ((bf16[8,3,64,2048]{3,2,1,0:T(8,128)(2,1)}), bf16[8,3,64,2048]{3,2,1,0:T(8,128)(2,1)}, u32[]{:S(2)}, u32[]{:S(2)}) async-start(bf16[8,3,64,2048]{3,2,1,0:T(8,128)(2,1)} %bitcast.104), calls=%async_computation | async-start | bytes 12582912 | tf_op jit(solution)/shard_map/all_to_all | solution.py:92
  42.7 0.7 subtract_bitcast_fusion
  43.4 2.5 convolution_convert_fusion.8
  46.3 3.5 %convolution_convert_fusion.2 = bf16[512,1024]{1,0:T(8,128)(2,1)} fusion(bf16[1024,1024]{1,0:T(8,128)(2,1)S(1)} %copy-done, bf16[512,1024]{1,0:T(8,128)(2,1)} %param.11, f32[1024]{0:T(1024)S(1)} %copy-done.16, f32[512]{0:T(512)S(1)} %add_rsqrt_fusion, f32[512]{0:T(512)S(1)} %broadcast_multiply_fusion), kind=kOutput, calls=%fused_computation.49 | convolution fusion | flops 1076887552 | bytes 4202496 | tf_op jit(solution)/shard_map/dot_general | solution.py:71
  49.9 2.3 copy.50
  52.2 1.3 copy.51
  53.5 4.0 %reshape.283 = bf16[8,64,16,64]{3,2,1,0:T(8,128)(2,1)} reshape(bf16[512,1024]{1,0:T(8,128)(2,1)} %convolution_convert_fusion.2) | data formatting | bytes 2097152 | tf_op jit(solution)/shard_map/reshape | solution.py:123
  57.5 71.0 %all-reduce.2.cloned.1.call-done = bf16[128,1024]{1,0:T(8,128)(2,1)} async-done(((bf16[128,1024]{1,0:T(8,128)(2,1)}), bf16[128,1024]{1,0:T(8,128)(2,1)}) %all-reduce.2.cloned.1.call-update) | async-done | bytes 262160 | tf_op jit(solution)/shard_map/psum | solution.py:105
  128.4 1.4 convolution_convert_fusion.7
  130.0 0.8 multiply_reduce_fusion.1
  130.9 1.2 fusion.10
  132.1 8.7 %all-gather.1 = f32[128,128]{1,0:T(8,128)S(1)} all-gather(f32[16,128]{1,0:T(8,128)S(1)} %fusion.10), channel_id=3, replica_groups=mesh['seq'=8,'dp'=4] {'seq'}, dimensions={0}, use_global_device_ids=true | all-gather | bytes 73728 | tf_op jit(solution)/shard_map/all_gather | solution.py:28
  140.8 8.9 %all-gather = f32[128,128]{1,0:T(8,128)S(1)} all-gather(f32[16,128]{1,0:T(8,128)S(1)} %get-tuple-element.102), channel_id=2, replica_groups=mesh['seq'=8,'dp'=4] {'seq'}, dimensions={0}, use_global_device_ids=true | all-gather | bytes 73728 | tf_op jit(solution)/shard_map/all_gather | solution.py:28
  149.8 4.0 %fusion.9 = f32[16,128,64]{1,2,0:T(8,128)} fusion(bf16[512,16,64]{0,2,1:T(8,128)(2,1)S(1)} %bitcast.111, f32[16,128,512]{2,1,0:T(8,128)S(1)} %get-tuple-element.103, f32[16,128]{1,0:T(8,128)S(1)} %get-tuple-element.102), kind=kOutput, calls=%fused_computation.22 | convolution fusion | flops 807403520 | bytes 5775360 | tf_op jit(solution)/shard_map/hqk,khd->hqd/dot_general | solution.py:145
  153.8 2.2 convolution_convert_fusion.5
  156.0 2.2 convolution_convert_fusion.6
  158.4 3.3 %pad_maximum_fusion.1 = bf16[8,3,64,2048]{3,2,1,0:T(8,128)(2,1)} fusion(bf16[8,1,64,2048]{3,2,1,0:T(8,128)(2,1)S(1)} %bitcast.110, bf16[8,1,64,2048]{3,2,1,0:T(8,128)(2,1)S(1)} %bitcast.102, bf16[8,1,64,2048]{3,2,1,0:T(8,128)(2,1)S(1)} %bitcast.109), kind=kLoop, calls=%fused_computation.19 | loop fusion | flops 6291456 | bytes 12582912 | tf_op jit(solution)/shard_map/stack | solution.py:79
  161.7 7.4 %gather_fusion.1 = bf16[24,64,2048]{2,1,0:T(8,128)(2,1)} fusion(bf16[24,64,2048]{2,1,0:T(8,128)(2,1)} %bitcast.23, s32[1024]{0:T(1024)S(1)} %pad_clamp_fusion), kind=kCustom, calls=%fused_computation.1 | custom fusion | bytes 12583008 | tf_op jit(solution)/shard_map/gather | solution.py:98
  169.0 0.5 broadcast_in_dim.22
  169.6 7.8 %pad_maximum_fusion = bf16[8,512,2048]{2,1,0:T(8,128)(2,1)S(1)} fusion(bf16[8,128,2048]{2,1,0:T(8,128)(2,1)S(1)} %broadcast_in_dim.22, bf16[8,192,2048]{2,1,0:T(8,128)(2,1)} %bitcast.106, bf16[8,192,2048]{2,1,0:T(8,128)(2,1)} %bitcast.105), kind=kLoop, calls=%fused_computation.12 | loop fusion | flops 50331648 | bytes 33554432 | tf_op jit(solution)/shard_map/concatenate | solution.py:119
  177.3 6.3 %fusion.53 = (bf16[8,512,1024]{2,1,0:T(8,128)(2,1)}, bf16[8,512,1024]{2,1,0:T(8,128)(2,1)}) fusion(bf16[8,512,2048]{2,1,0:T(8,128)(2,1)S(1)} %pad_maximum_fusion), kind=kLoop, calls=%fused_computation.113 | loop fusion | bytes 33554432 | tf_op jit(solution)/shard_map/slice | solution.py:121
  183.6 11.5 %copy.61 = bf16[8,512,1024]{1,2,0:T(8,128)(2,1)} copy(bf16[8,512,1024]{2,1,0:T(8,128)(2,1)} %get-tuple-element.93) | data formatting | bytes 16777216 | tf_op jit(solution)/shard_map/slice | solution.py:121
  195.1 11.6 %copy.60 = bf16[8,512,1024]{1,2,0:T(8,128)(2,1)} copy(bf16[8,512,1024]{2,1,0:T(8,128)(2,1)} %get-tuple-element.94) | data formatting | bytes 16777216 | tf_op jit(solution)/shard_map/slice | solution.py:122
  206.7 10.5 %fusion.54 = (f32[8,16,64]{2,1,0:T(8,128)S(1)}, f32[8,16,64,512]{3,2,1,0:T(8,128)}) fusion(bf16[8,512,16,64]{1,3,2,0:T(8,128)(2,1)} %bitcast.103, bf16[8,64,16,64]{3,2,1,0:T(8,128)(2,1)S(1)} %copy-done.6), kind=kOutput, calls=%fused_computation.114 | convolution fusion | flops 549454336 | bytes 26247168 | tf_op jit(solution)/shard_map/sub | solution.py:129
  217.1 10.9 %convert_bitcast_fusion = bf16[8,64,16,64]{1,3,2,0:T(8,128)(2,1)} fusion(bf16[8,512,16,64]{1,3,2,0:T(8,128)(2,1)} %bitcast.108, f32[8,16,64,512]{3,2,1,0:T(8,128)} %get-tuple-element.101, f32[8,16,64]{2,1,0:T(8,128)S(1)} %get-tuple-element.100), kind=kOutput, calls=%fused_computation.41 | convolution fusion | flops 545783808 | bytes 26247168 | tf_op jit(solution)/shard_map/bhqk,bkhd->bqhd/dot_general | solution.py:131
  228.1 3.6 %copy.63 = bf16[8,64,16,64]{3,2,1,0:T(8,128)(2,1)S(1)} copy(bf16[8,64,16,64]{1,3,2,0:T(8,128)(2,1)} %convert_bitcast_fusion) | data formatting | bytes 2097152 | tf_op jit(solution)/shard_map/convert_element_type | solution.py:134
  231.7 2.3 convert_element_type.95
  234.0 1.1 slice.66
  235.1 0.3 copy.52
  235.4 4.3 %slice.69 = f32[112,128,64]{1,2,0:T(8,128)} slice(f32[128,128,64]{1,2,0:T(8,128)} %all-gather.5.cloned.1.call-done), slice={[16:128], [0:128], [0:64]} | slice | bytes 7340032 | tf_op jit(solution)/shard_map/slice | solution.py:30
  239.8 17.1 %while.14 = (s32[]{:T(128)}, f32[16,128]{1,0:T(8,128)S(1)}, f32[16,128]{1,0:T(8,128)S(1)}, f32[16,128,64]{2,1,0:T(8,128)S(1)}, f32[7,16,128]{2,1,0:T(8,128)S(1)}...) while((s32[]{:T(128)}, f32[16,128]{1,0:T(8,128)S(1)}, f32[16,128]{1,0:T(8,128)S(1)}, ...), condition=%wide.region_7.8_spmd, body=%wide.region_6.7_spmd.sunk | while | flops 405506 | bytes 3752029 | solution.py:31
  239.8 1.1 constant_dynamic-slice_fusion.3
  240.9 0.3 copy.78
  241.2 1.0 fusion.79
  242.2 1.1 constant_dynamic-slice_fusion.3
  243.3 0.3 copy.78
  243.7 1.0 fusion.79
  244.7 1.1 constant_dynamic-slice_fusion.3
  245.8 0.3 copy.78
  246.1 1.0 fusion.79
  247.1 1.1 constant_dynamic-slice_fusion.3
  248.2 0.3 copy.78
  248.5 1.0 fusion.79
  249.6 1.1 constant_dynamic-slice_fusion.3
  250.6 0.3 copy.78
  251.0 1.0 fusion.79
  252.0 1.1 constant_dynamic-slice_fusion.3
  253.1 0.3 copy.78
  253.4 1.0 fusion.79
  254.5 1.1 constant_dynamic-slice_fusion.3
  255.9 1.0 fusion.79
  257.3 0.8 copy-done.12
  258.1 4.2 %convolution_convert_fusion.1 = bf16[512,1024]{1,0:T(8,128)(2,1)} fusion(bf16[1024,1024]{1,0:T(8,128)(2,1)} %param.16, bf16[512,1024]{1,0:T(8,128)(2,1)S(1)} %copy-done.12, bf16[128,1024]{0,1:T(8,128)(2,1)S(1)} %bitcast.114, pred[512]{0:T(512)(128)(4,1)S(1)} %broadcast_compare_fusion.1, s32[128]{0:T(128)S(1)} %subtract_bitcast_fusion), kind=kOutput, calls=%fused_computation.48 | convolution fusion | flops 1209663488 | bytes 4457472 | tf_op jit(solution)/shard_map/dot_general | solution.py:156
  (76 shorter events, 2.4 us)
Async XLA Ops:
  6.5 39.8 %copy-start = (bf16[1024,1024]{1,0:T(8,128)(2,1)S(1)}, bf16[1024,1024]{1,0:T(8,128)(2,1)}, u32[]{:S(2)}) copy-start(bf16[1024,1024]{1,0:T(8,128)(2,1)} %param.13) | copy-start | bytes 6291460
  6.5 3.2 %copy-start.7 = (bf16[512,1024]{1,0:T(8,128)(2,1)S(1)}, bf16[512,1024]{1,0:T(8,128)(2,1)}, u32[]{:S(2)}) copy-start(bf16[512,1024]{1,0:T(8,128)(2,1)} %param.11) | copy-start | bytes 3145732
  6.5 3.3 %copy-start.16 = (f32[1024]{0:T(1024)S(1)}, f32[1024]{0:T(1024)}, u32[]{:S(2)}) copy-start(f32[1024]{0:T(1024)} %param.12) | copy-start | bytes 12292
  9.8 3.1 %copy-start.11 = (bf16[1024,1024]{1,0:T(8,128)(2,1)S(1)}, bf16[1024,1024]{1,0:T(8,128)(2,1)}, u32[]{:S(2)}) copy-start(bf16[1024,1024]{1,0:T(8,128)(2,1)} %param.15) | copy-start | bytes 6291460
  12.9 1.4 copy-start.3
  14.3 4.2 %copy-start.15 = (s32[64,3]{0,1:T(4,128)S(1)}, s32[64,3]{0,1:T(4,128)}, u32[]{:S(2)}) copy-start(s32[64,3]{0,1:T(4,128)} %param.17) | copy-start | bytes 2308
  15.1 7.7 %collective-permute-start = (bf16[64,2048]{1,0:T(8,128)(2,1)}, bf16[64,2048]{1,0:T(8,128)(2,1)S(1)}, u32[]{:S(2)}, u32[]{:S(2)}) collective-permute-start(bf16[64,2048]{1,0:T(8,128)(2,1)} %get-tuple-element.98), channel_id=1, source_target_pairs={{0,4},{4,8},{8,12},{12,16},{16,20},{20,24},{24,28},{28,0},{1,5},{5... | collective-permute-start | bytes 786440 | tf_op jit(solution)/shard_map/ppermute | solution.py:19
  15.6 8.9 %collective-permute-start.1 = (bf16[64,2048]{1,0:T(8,128)(2,1)}, bf16[64,2048]{1,0:T(8,128)(2,1)}, u32[]{:S(2)}, u32[]{:S(2)}) collective-permute-start(bf16[64,2048]{1,0:T(8,128)(2,1)} %get-tuple-element.99), channel_id=1, source_target_pairs={{4,0},{8,4},{12,8},{16,12},{20,16},{24,20},{28,24},{0,28},{5,1},{9... | collective-permute-start | bytes 786440 | tf_op jit(solution)/shard_map/ppermute | solution.py:22
  37.2 124.4 %all-to-all-start = ((bf16[8,3,64,2048]{3,2,1,0:T(8,128)(2,1)}), bf16[8,3,64,2048]{3,2,1,0:T(8,128)(2,1)}, u32[]{:S(2)}, u32[]{:S(2)}) async-start(bf16[8,3,64,2048]{3,2,1,0:T(8,128)(2,1)} %bitcast.104), calls=%async_computation | async-start | bytes 12582912 | tf_op jit(solution)/shard_map/all_to_all | solution.py:92
  42.0 86.5 %all-reduce.2.cloned.1.call-start = ((), (), s32[]{:S(2)}) async-start(), calls=%async_computation.1 | async-start | bytes 524288 | tf_op jit(solution)/shard_map/psum | solution.py:105
  45.9 188.0 %all-gather.5.cloned.1.call-start = ((), (), s32[]{:S(2)}) async-start(), calls=%async_computation.2 | async-start | bytes 4718592 | tf_op jit(solution)/shard_map/all_gather | solution.py:28
  57.5 72.5 %copy-start.9 = (bf16[512,1024]{0,1:T(8,128)(2,1)S(1)}, bf16[512,1024]{0,1:T(8,128)(2,1)}, u32[]{:S(2)}) copy-start(bf16[512,1024]{0,1:T(8,128)(2,1)} %copy.50) | copy-start | bytes 3145732
  130.9 18.9 %copy-start.8 = (bf16[512,1024]{0,1:T(8,128)(2,1)S(1)}, bf16[512,1024]{0,1:T(8,128)(2,1)}, u32[]{:S(2)}) copy-start(bf16[512,1024]{0,1:T(8,128)(2,1)} %copy.51) | copy-start | bytes 3145732
  140.8 17.4 %copy-start.13 = (f32[128,128]{1,0:T(8,128)}, f32[128,128]{1,0:T(8,128)S(1)}, u32[]{:S(2)}) copy-start(f32[128,128]{1,0:T(8,128)S(1)} %all-gather.1) | copy-start | bytes 196612
  149.8 8.5 %copy-start.14 = (f32[128,128]{1,0:T(8,128)}, f32[128,128]{1,0:T(8,128)S(1)}, u32[]{:S(2)}) copy-start(f32[128,128]{1,0:T(8,128)S(1)} %all-gather) | copy-start | bytes 196612
  149.8 4.0 %copy-start.10 = (bf16[128,1024]{1,0:T(8,128)(2,1)S(1)}, bf16[128,1024]{1,0:T(8,128)(2,1)}, u32[]{:S(2)}) copy-start(bf16[128,1024]{1,0:T(8,128)(2,1)} %all-reduce.2.cloned.1.call-done) | copy-start | bytes 786436
  153.8 4.5 %copy-start.4 = (bf16[512,2048]{1,0:T(8,128)(2,1)S(1)}, bf16[512,2048]{1,0:T(8,128)(2,1)}, u32[]{:S(2)}) copy-start(bf16[512,2048]{1,0:T(8,128)(2,1)} %get-tuple-element.95) | copy-start | bytes 6291460
  153.8 4.5 %copy-start.5 = (bf16[512,2048]{1,0:T(8,128)(2,1)S(1)}, bf16[512,2048]{1,0:T(8,128)(2,1)}, u32[]{:S(2)}) copy-start(bf16[512,2048]{1,0:T(8,128)(2,1)} %get-tuple-element.96) | copy-start | bytes 6291460
  156.0 2.4 copy-start.2
  195.1 11.6 %copy-start.6 = (bf16[8,64,16,64]{3,2,1,0:T(8,128)(2,1)S(1)}, bf16[8,64,16,64]{3,2,1,0:T(8,128)(2,1)}, u32[]{:S(2)}) copy-start(bf16[8,64,16,64]{3,2,1,0:T(8,128)(2,1)} %reshape.283) | copy-start | bytes 3145732
  235.4 4.4 %slice-start = ((f32[128,128]{1,0:T(8,128)}), f32[16,128]{1,0:T(8,128)S(1)}, s32[]{:S(2)}) async-start(f32[128,128]{1,0:T(8,128)} %copy-done.13), calls=%async_computation.3 | async-start | bytes 16384 | tf_op jit(solution)/shard_map/slice | solution.py:29
  235.4 4.3 %slice-start.1 = ((f32[128,128]{1,0:T(8,128)}), f32[16,128]{1,0:T(8,128)S(1)}, s32[]{:S(2)}) async-start(f32[128,128]{1,0:T(8,128)} %copy-done.14), calls=%async_computation.4 | async-start | bytes 16384 | tf_op jit(solution)/shard_map/slice | solution.py:29
  256.9 1.2 copy-start.12
  257.3 5.1 %copy-start.1 = (bf16[1024,1024]{1,0:T(8,128)(2,1)S(1)}, bf16[1024,1024]{1,0:T(8,128)(2,1)}, u32[]{:S(2)}) copy-start(bf16[1024,1024]{1,0:T(8,128)(2,1)} %param.13) | copy-start | bytes 6291460
Sparse Core Ops, SparseCore 0:
  46.0 82.3 all-reduce.1
  153.9 36.7 all-gather.4
where the time goes:
time: 271 us; the launch traced here: 269 us
  waiting for transfers between devices  76.3 us (28%)
  local copies, waits for them, and re-layouts  74.2 us (27%)
  matrix products  46.6 us (17%)
  other arithmetic  31.5 us (12%)
  blocking collectives  17.6 us (6%)
  between operations  14.4 us (5%)
  starting transfers between devices  8.15 us (3%)
    psum x1, waiting for transfers between devices, body(): lax.psum(jnp.dot(selector, normed, preferred_element_type=jnp.float32).as...  71 us
    slice x2, local copies, waits for them, and re-layouts, body(): key_part = key_set[:, :, :width].reshape(local_blocks, count, HEADS, HDIM)  17.8 us
    all_gather x2, blocking collectives, combined_all(): pieces = jax.tree.map(lambda part: lax.all_gather(part, axis), value)  17.6 us
    slice x1, local copies, waits for them, and re-layouts, body(): value_part = key_set[:, :, width:].reshape(local_blocks, count, HEADS, HDIM)  11.6 us
    dot_general x1, matrix products, body(): jnp.einsum('bhqk,bkhd->bqhd', probs, value_part, preferred_element_type=j...  10.9 us
    sub x1, matrix products, body(): expo = jnp.exp(scores - top_score)  10.5 us
    dynamic_slice x14, local copies, waits for them, and re-layouts, combined_all(): lax.scan(lambda running, piece: (join(running, piece), None), head, tail)  9.93 us
    concatenate x1, other arithmetic, body(): key_set = jnp.concatenate([window, random_rows, global_broad], axis=1)  7.77 us
  transfers between devices with their start and end apart: 5, of which 3 were waited for; matrix products, arithmetic and copies ran while one was open for 38% of the time, Pallas kernels for 0%

commit v1 on v0

--- a/solution.py
+++ b/solution.py
@@ -102,9 +102,8 @@
     selector = (local_position[:, None] == jnp.arange(rows_here, dtype=jnp.int32)[None, :]).astype(
         jnp.bfloat16
     )
-    global_normed = lax.psum(
-        jnp.dot(selector, normed, preferred_element_type=jnp.float32).astype(jnp.bfloat16), "seq"
-    )
+    u_in = jnp.dot(selector, normed, preferred_element_type=jnp.float32).astype(jnp.bfloat16)
+    global_normed = jnp.sum(lax.all_gather(u_in, "seq"), 0)
     global_queries = jnp.dot(
         global_normed, query_weight, preferred_element_type=jnp.float32
     ).astype(jnp.bfloat16)

time: 271 us -> 247 us (0.911)
  waiting for transfers between devices: 76.3 us -> 8.17 us
  blocking collectives: 17.6 us -> 61.8 us
  matrix products: 46.6 us -> 42.4 us
  other arithmetic: 31.5 us -> 35.7 us
    psum x1 -> x0, waiting for transfers between devices: 71 us -> none  [body(): lax.psum(jnp.dot(selector, normed, preferred_element_type=jnp.float32).as...]
    all_gather x2, blocking collectives: 17.6 us -> 61.8 us  [combined_all(): pieces = jax.tree.map(lambda part: lax.all_gather(part, axis), value)]
    another operation x1, other arithmetic: 3.27 us -> 6.13 us  [body(): jnp.stack([wide_blocks[:-2], wide_blocks[1:-1], wide_blocks[2:]], axis=1)]
    ppermute x1, waiting for transfers between devices: 1.65 us -> 4.45 us  [with_halo(): lax.ppermute(lax.slice_in_dim(block, 0, width, axis=dim), axis, backward)]
  transfers between devices with their start and end apart: 5 -> 5, of which waited for: 3 -> 2; matrix products, arithmetic and copies ran while one was open for 38% -> 48% of each run, Pallas kernels for 0% -> 0%
where the time goes in v1:
time: 247 us; the launch traced here: 245 us
  local copies, waits for them, and re-layouts  73.8 us (30%)
  blocking collectives  61.8 us (25%)
  matrix products  42.4 us (17%)
  other arithmetic  35.7 us (14%)
  between operations  14.5 us (6%)
  starting transfers between devices  8.32 us (3%)
  waiting for transfers between devices  8.17 us (3%)
    all_gather x2, blocking collectives, combined_all(): pieces = jax.tree.map(lambda part: lax.all_gather(part, axis), value)  61.8 us
    slice x2, local copies, waits for them, and re-layouts, body(): key_part = key_set[:, :, :width].reshape(local_blocks, count, HEADS, HDIM)  18 us
    slice x1, local copies, waits for them, and re-layouts, body(): value_part = key_set[:, :, width:].reshape(local_blocks, count, HEADS, HDIM)  11.6 us
    dot_general x1, matrix products, body(): jnp.einsum('bhqk,bkhd->bqhd', probs, value_part, preferred_element_type=j...  10.9 us
    sub x1, matrix products, body(): expo = jnp.exp(scores - top_score)  10.5 us
    dynamic_slice x14, local copies, waits for them, and re-layouts, combined_all(): lax.scan(lambda running, piece: (join(running, piece), None), head, tail)  9.93 us
    gather x1, local copies, waits for them, and re-layouts, body(): random_rows = incoming[my_source * capacity + my_rank]  7.5 us
    concatenate x1, other arithmetic, body(): key_set = jnp.concatenate([window, random_rows, global_broad], axis=1)  7.25 us
  transfers between devices with their start and end apart: 5, of which 2 were waited for; matrix products, arithmetic and copies ran while one was open for 48% of the time, Pallas kernels for 0%

profile of v1, /device:TPU:0, one launch (start us, length us, event | category | flops | bytes accessed | tf_op | source)
XLA Modules:
  0.0 244.9 jit_solution(10250483867918517514)
XLA Ops:
  7.3 1.5 convert_reduce_fusion
  8.9 1.6 fusion.15
  10.5 0.7 subtract_bitcast_fusion
  11.2 1.3 convolution_convert_fusion.8
  12.5 3.0 %convolution_convert_fusion.4 = bf16[512,1024]{1,0:T(8,128)(2,1)S(1)} fusion(bf16[1024,1024]{1,0:T(8,128)(2,1)} %param.14, bf16[512,1024]{1,0:T(8,128)(2,1)S(1)} %copy-done.4, f32[1024]{0:T(1024)S(1)} %copy-done.14, f32[512]{0:T(512)S(1)} %add_rsqrt_fusion, f32[512]{0:T(512)S(1)} %broadcast_multiply_fusion), kind=kOutput, calls=%fused_computation.51 | convolution fusion | flops 1076887552 | bytes 4202496 | tf_op jit(solution)/shard_map/dot_general | solution.py:72
  15.6 1.3 convolution_convert_fusion.3
  17.0 0.8 fusion.29
  17.8 0.5 collective-permute-start
  18.3 2.9 %collective-permute-start.1 = (bf16[64,2048]{1,0:T(8,128)(2,1)}, bf16[64,2048]{1,0:T(8,128)(2,1)}, u32[]{:S(2)}, u32[]{:S(2)}) collective-permute-start(bf16[64,2048]{1,0:T(8,128)(2,1)} %get-tuple-element.99), channel_id=1, source_target_pairs={{4,0},{8,4},{12,8},{16,12},{20,16},{24,20},{28,24},{0,28},{5,1},{9... | collective-permute-start | bytes 786440 | tf_op jit(solution)/shard_map/ppermute | solution.py:22
  21.9 3.7 %collective-permute-done = bf16[64,2048]{1,0:T(8,128)(2,1)S(1)} collective-permute-done((bf16[64,2048]{1,0:T(8,128)(2,1)}, bf16[64,2048]{1,0:T(8,128)(2,1)S(1)}, u32[]{:S(2)}, u32[]{:S(2)}) %collective-permute-start) | collective-permute-done | bytes 262176 | tf_op jit(solution)/shard_map/ppermute | solution.py:19
  25.6 4.4 %collective-permute-done.1 = bf16[64,2048]{1,0:T(8,128)(2,1)} collective-permute-done((bf16[64,2048]{1,0:T(8,128)(2,1)}, bf16[64,2048]{1,0:T(8,128)(2,1)}, u32[]{:S(2)}, u32[]{:S(2)}) %collective-permute-start.1) | collective-permute-done | bytes 262176 | tf_op jit(solution)/shard_map/ppermute | solution.py:22
  30.0 6.7 %pad_maximum_fusion.5 = (bf16[512,2048]{1,0:T(8,128)(2,1)}, bf16[512,2048]{1,0:T(8,128)(2,1)}, bf16[512,2048]{1,0:T(8,128)(2,1)}) fusion(bf16[64,2048]{1,0:T(8,128)(2,1)S(1)} %collective-permute-done, bf16[512,1024]{1,0:T(8,128)(2,1)S(1)} %convolution_convert_fusion.3, bf16[512,1024]{1,0:T(8,128)(2,1)} %copy-done.2, bf16[64,2048]{1,0:T(8,128)(2,1)} %collective-permute-done.1), kind=kLoop, calls=%fused_computation.39 | loop fusion | flops 16777216 | bytes 8912896 | tf_op jit(solution)/shard_map/concatenate | solution.py:23
  36.7 6.1 %gather_fusion = bf16[24,64,2048]{2,1,0:T(8,128)(2,1)} fusion(bf16[8,64,2048]{2,1,0:T(8,128)(2,1)} %bitcast.102, s32[1024]{0:T(1024)S(1)} %pad_clamp_fusion.1), kind=kCustom, calls=%fused_computation | custom fusion | bytes 12583008 | tf_op jit(solution)/shard_map/gather | solution.py:91
  42.8 4.8 %all-to-all-start = ((bf16[8,3,64,2048]{3,2,1,0:T(8,128)(2,1)}), bf16[8,3,64,2048]{3,2,1,0:T(8,128)(2,1)}, u32[]{:S(2)}, u32[]{:S(2)}) async-start(bf16[8,3,64,2048]{3,2,1,0:T(8,128)(2,1)} %bitcast.105), calls=%async_computation | async-start | bytes 12582912 | tf_op jit(solution)/shard_map/all_to_all | solution.py:92
  47.8 2.3 copy.50
  50.1 1.3 copy.51
  51.4 2.5 %convolution_convert_fusion.2 = bf16[512,1024]{1,0:T(8,128)(2,1)S(1)} fusion(bf16[1024,1024]{1,0:T(8,128)(2,1)S(1)} %copy-done, bf16[512,1024]{1,0:T(8,128)(2,1)} %param.11, f32[1024]{0:T(1024)S(1)} %copy-done.14, f32[512]{0:T(512)S(1)} %add_rsqrt_fusion, f32[512]{0:T(512)S(1)} %broadcast_multiply_fusion), kind=kOutput, calls=%fused_computation.49 | convolution fusion | flops 1076887552 | bytes 4202496 | tf_op jit(solution)/shard_map/dot_general | solution.py:71
  53.9 2.3 reshape.283
  56.6 6.1 %pad_maximum_fusion.1 = bf16[8,3,64,2048]{3,2,1,0:T(8,128)(2,1)} fusion(bf16[8,1,64,2048]{3,2,1,0:T(8,128)(2,1)} %bitcast.111, bf16[8,1,64,2048]{3,2,1,0:T(8,128)(2,1)} %bitcast.103, bf16[8,1,64,2048]{3,2,1,0:T(8,128)(2,1)} %bitcast.110), kind=kLoop, calls=%fused_computation.19 | loop fusion | flops 6291456 | bytes 12582912 | tf_op jit(solution)/shard_map/stack | solution.py:79
  62.7 2.0 reduce_sum.82
  64.7 1.1 convolution_convert_fusion.7
  65.8 1.1 copy.49
  67.0 0.8 multiply_reduce_fusion.1
  67.8 1.2 fusion.10
  69.0 53.5 %all-gather.2 = f32[128,128]{1,0:T(8,128)S(1)} all-gather(f32[16,128]{1,0:T(8,128)S(1)} %fusion.10), channel_id=4, replica_groups=mesh['seq'=8,'dp'=4] {'seq'}, dimensions={0}, use_global_device_ids=true | all-gather | bytes 73728 | tf_op jit(solution)/shard_map/all_gather | solution.py:28
  122.6 8.3 %all-gather.1 = f32[128,128]{1,0:T(8,128)S(1)} all-gather(f32[16,128]{1,0:T(8,128)S(1)} %get-tuple-element.102), channel_id=3, replica_groups=mesh['seq'=8,'dp'=4] {'seq'}, dimensions={0}, use_global_device_ids=true | all-gather | bytes 73728 | tf_op jit(solution)/shard_map/all_gather | solution.py:28
  130.8 4.0 %fusion.9 = f32[16,128,64]{1,2,0:T(8,128)} fusion(bf16[512,16,64]{0,2,1:T(8,128)(2,1)S(1)} %bitcast.112, f32[16,128,512]{2,1,0:T(8,128)S(1)} %get-tuple-element.103, f32[16,128]{1,0:T(8,128)S(1)} %get-tuple-element.102), kind=kOutput, calls=%fused_computation.22 | convolution fusion | flops 807403520 | bytes 5775360 | tf_op jit(solution)/shard_map/hqk,khd->hqd/dot_general | solution.py:144
  134.8 2.2 convolution_convert_fusion.5
  137.0 0.5 convolution_convert_fusion.6
  137.6 7.5 %gather_fusion.1 = bf16[24,64,2048]{2,1,0:T(8,128)(2,1)} fusion(bf16[24,64,2048]{2,1,0:T(8,128)(2,1)} %bitcast.24, s32[1024]{0:T(1024)S(1)} %pad_clamp_fusion), kind=kCustom, calls=%fused_computation.1 | custom fusion | bytes 12583008 | tf_op jit(solution)/shard_map/gather | solution.py:98
  145.1 0.5 broadcast_in_dim.22
  145.6 7.3 %pad_maximum_fusion = bf16[8,512,2048]{2,1,0:T(8,128)(2,1)S(1)} fusion(bf16[8,128,2048]{2,1,0:T(8,128)(2,1)S(1)} %broadcast_in_dim.22, bf16[8,192,2048]{2,1,0:T(8,128)(2,1)} %bitcast.107, bf16[8,192,2048]{2,1,0:T(8,128)(2,1)} %bitcast.106), kind=kLoop, calls=%fused_computation.12 | loop fusion | flops 50331648 | bytes 33554432 | tf_op jit(solution)/shard_map/concatenate | solution.py:118
  152.9 6.4 %fusion.53 = (bf16[8,512,1024]{2,1,0:T(8,128)(2,1)}, bf16[8,512,1024]{2,1,0:T(8,128)(2,1)}) fusion(bf16[8,512,2048]{2,1,0:T(8,128)(2,1)S(1)} %pad_maximum_fusion), kind=kLoop, calls=%fused_computation.113 | loop fusion | bytes 33554432 | tf_op jit(solution)/shard_map/slice | solution.py:120
  159.2 11.6 %copy.61 = bf16[8,512,1024]{1,2,0:T(8,128)(2,1)} copy(bf16[8,512,1024]{2,1,0:T(8,128)(2,1)} %get-tuple-element.93) | data formatting | bytes 16777216 | tf_op jit(solution)/shard_map/slice | solution.py:120
  170.8 11.6 %copy.60 = bf16[8,512,1024]{1,2,0:T(8,128)(2,1)} copy(bf16[8,512,1024]{2,1,0:T(8,128)(2,1)} %get-tuple-element.94) | data formatting | bytes 16777216 | tf_op jit(solution)/shard_map/slice | solution.py:121
  182.5 10.5 %fusion.54 = (f32[8,16,64]{2,1,0:T(8,128)S(1)}, f32[8,16,64,512]{3,2,1,0:T(8,128)}) fusion(bf16[8,512,16,64]{1,3,2,0:T(8,128)(2,1)} %bitcast.104, bf16[8,64,16,64]{3,2,1,0:T(8,128)(2,1)S(1)} %copy-done.3), kind=kOutput, calls=%fused_computation.114 | convolution fusion | flops 549454336 | bytes 26247168 | tf_op jit(solution)/shard_map/sub | solution.py:128
  192.9 10.9 %convert_bitcast_fusion = bf16[8,64,16,64]{1,3,2,0:T(8,128)(2,1)} fusion(bf16[8,512,16,64]{1,3,2,0:T(8,128)(2,1)} %bitcast.109, f32[8,16,64,512]{3,2,1,0:T(8,128)} %get-tuple-element.101, f32[8,16,64]{2,1,0:T(8,128)S(1)} %get-tuple-element.100), kind=kOutput, calls=%fused_computation.41 | convolution fusion | flops 545783808 | bytes 26247168 | tf_op jit(solution)/shard_map/bhqk,bkhd->bqhd/dot_general | solution.py:130
  203.8 3.6 %copy.63 = bf16[8,64,16,64]{3,2,1,0:T(8,128)(2,1)S(1)} copy(bf16[8,64,16,64]{1,3,2,0:T(8,128)(2,1)} %convert_bitcast_fusion) | data formatting | bytes 2097152 | tf_op jit(solution)/shard_map/convert_element_type | solution.py:133
  207.5 2.3 convert_element_type.97
  209.7 1.1 slice.66
  210.8 0.3 copy.52
  211.2 4.3 %slice.69 = f32[112,128,64]{1,2,0:T(8,128)} slice(f32[128,128,64]{1,2,0:T(8,128)} %all-gather.9.cloned.1.call-done), slice={[16:128], [0:128], [0:64]} | slice | bytes 7340032 | tf_op jit(solution)/shard_map/slice | solution.py:30
  215.5 17.1 %while.14 = (s32[]{:T(128)}, f32[16,128]{1,0:T(8,128)S(1)}, f32[16,128]{1,0:T(8,128)S(1)}, f32[16,128,64]{2,1,0:T(8,128)S(1)}, f32[7,16,128]{2,1,0:T(8,128)S(1)}...) while((s32[]{:T(128)}, f32[16,128]{1,0:T(8,128)S(1)}, f32[16,128]{1,0:T(8,128)S(1)}, ...), condition=%wide.region_7.8_spmd, body=%wide.region_6.7_spmd.sunk | while | flops 405506 | bytes 3752029 | solution.py:31
  215.6 1.1 constant_dynamic-slice_fusion.3
  216.6 0.3 copy.78
  217.0 1.0 fusion.79
  218.0 1.1 constant_dynamic-slice_fusion.3
  219.1 0.3 copy.78
  219.4 1.0 fusion.79
  220.4 1.1 constant_dynamic-slice_fusion.3
  221.5 0.3 copy.78
  221.9 1.0 fusion.79
  222.9 1.1 constant_dynamic-slice_fusion.3
  224.0 0.3 copy.78
  224.3 1.0 fusion.79
  225.3 1.1 constant_dynamic-slice_fusion.3
  226.4 0.3 copy.78
  226.8 1.0 fusion.79
  227.8 1.1 constant_dynamic-slice_fusion.3
  229.2 1.0 fusion.79
  230.2 1.1 constant_dynamic-slice_fusion.3
  231.7 1.0 fusion.79
  233.1 0.8 copy-done.10
  233.9 4.2 %convolution_convert_fusion.1 = bf16[512,1024]{1,0:T(8,128)(2,1)} fusion(bf16[1024,1024]{1,0:T(8,128)(2,1)} %param.16, bf16[512,1024]{1,0:T(8,128)(2,1)S(1)} %copy-done.10, bf16[128,1024]{0,1:T(8,128)(2,1)S(1)} %bitcast.116, pred[512]{0:T(512)(128)(4,1)S(1)} %broadcast_compare_fusion.1, s32[128]{0:T(128)S(1)} %subtract_bitcast_fusion), kind=kOutput, calls=%fused_computation.48 | convolution fusion | flops 1209663488 | bytes 4457472 | tf_op jit(solution)/shard_map/dot_general | solution.py:155
  (73 shorter events, 2.6 us)
Async XLA Ops:
  6.5 44.8 %copy-start = (bf16[1024,1024]{1,0:T(8,128)(2,1)S(1)}, bf16[1024,1024]{1,0:T(8,128)(2,1)}, u32[]{:S(2)}) copy-start(bf16[1024,1024]{1,0:T(8,128)(2,1)} %param.13) | copy-start | bytes 6291460
  6.5 4.7 %copy-start.4 = (bf16[512,1024]{1,0:T(8,128)(2,1)S(1)}, bf16[512,1024]{1,0:T(8,128)(2,1)}, u32[]{:S(2)}) copy-start(bf16[512,1024]{1,0:T(8,128)(2,1)} %param.11) | copy-start | bytes 3145732
  6.5 4.7 %copy-start.14 = (f32[1024]{0:T(1024)S(1)}, f32[1024]{0:T(1024)}, u32[]{:S(2)}) copy-start(f32[1024]{0:T(1024)} %param.12) | copy-start | bytes 12292
  6.5 56.2 %all-gather.7.cloned.1.call-start = ((), (), s32[]{:S(2)}) async-start(), calls=%async_computation.1 | async-start | bytes 2359296 | tf_op jit(solution)/shard_map/all_gather | solution.py:106
  12.5 3.1 %copy-start.5 = (bf16[512,1024]{1,0:T(8,128)(2,1)S(1)}, bf16[512,1024]{1,0:T(8,128)(2,1)}, u32[]{:S(2)}) copy-start(bf16[512,1024]{1,0:T(8,128)(2,1)} %param.11) | copy-start | bytes 3145732
  12.5 3.1 %copy-start.8 = (bf16[1024,1024]{1,0:T(8,128)(2,1)S(1)}, bf16[1024,1024]{1,0:T(8,128)(2,1)}, u32[]{:S(2)}) copy-start(bf16[1024,1024]{1,0:T(8,128)(2,1)} %param.15) | copy-start | bytes 6291460
  15.6 1.4 copy-start.2
  17.0 4.2 %copy-start.13 = (s32[64,3]{0,1:T(4,128)S(1)}, s32[64,3]{0,1:T(4,128)}, u32[]{:S(2)}) copy-start(s32[64,3]{0,1:T(4,128)} %param.17) | copy-start | bytes 2308
  17.8 7.7 %collective-permute-start = (bf16[64,2048]{1,0:T(8,128)(2,1)}, bf16[64,2048]{1,0:T(8,128)(2,1)S(1)}, u32[]{:S(2)}, u32[]{:S(2)}) collective-permute-start(bf16[64,2048]{1,0:T(8,128)(2,1)} %get-tuple-element.98), channel_id=1, source_target_pairs={{0,4},{4,8},{8,12},{12,16},{16,20},{20,24},{24,28},{28,0},{1,5},{5... | collective-permute-start | bytes 786440 | tf_op jit(solution)/shard_map/ppermute | solution.py:19
  18.3 11.7 %collective-permute-start.1 = (bf16[64,2048]{1,0:T(8,128)(2,1)}, bf16[64,2048]{1,0:T(8,128)(2,1)}, u32[]{:S(2)}, u32[]{:S(2)}) collective-permute-start(bf16[64,2048]{1,0:T(8,128)(2,1)} %get-tuple-element.99), channel_id=1, source_target_pairs={{4,0},{8,4},{12,8},{16,12},{20,16},{24,20},{28,24},{0,28},{5,1},{9... | collective-permute-start | bytes 786440 | tf_op jit(solution)/shard_map/ppermute | solution.py:22
  42.8 94.8 %all-to-all-start = ((bf16[8,3,64,2048]{3,2,1,0:T(8,128)(2,1)}), bf16[8,3,64,2048]{3,2,1,0:T(8,128)(2,1)}, u32[]{:S(2)}, u32[]{:S(2)}) async-start(bf16[8,3,64,2048]{3,2,1,0:T(8,128)(2,1)} %bitcast.105), calls=%async_computation | async-start | bytes 12582912 | tf_op jit(solution)/shard_map/all_to_all | solution.py:92
  47.6 162.2 %all-gather.9.cloned.1.call-start = ((), (), s32[]{:S(2)}) async-start(), calls=%async_computation.2 | async-start | bytes 4718592 | tf_op jit(solution)/shard_map/all_gather | solution.py:28
  64.7 2.3 copy-start.7
  67.8 63.0 %copy-start.6 = (bf16[512,1024]{0,1:T(8,128)(2,1)S(1)}, bf16[512,1024]{0,1:T(8,128)(2,1)}, u32[]{:S(2)}) copy-start(bf16[512,1024]{0,1:T(8,128)(2,1)} %copy.51) | copy-start | bytes 3145732
  122.6 15.0 %copy-start.11 = (f32[128,128]{1,0:T(8,128)}, f32[128,128]{1,0:T(8,128)S(1)}, u32[]{:S(2)}) copy-start(f32[128,128]{1,0:T(8,128)S(1)} %all-gather.2) | copy-start | bytes 196612
  130.8 6.7 %copy-start.12 = (f32[128,128]{1,0:T(8,128)}, f32[128,128]{1,0:T(8,128)S(1)}, u32[]{:S(2)}) copy-start(f32[128,128]{1,0:T(8,128)S(1)} %all-gather.1) | copy-start | bytes 196612
  134.8 2.2 copy-start.9
  170.8 11.6 %copy-start.3 = (bf16[8,64,16,64]{3,2,1,0:T(8,128)(2,1)S(1)}, bf16[8,64,16,64]{3,2,1,0:T(8,128)(2,1)}, u32[]{:S(2)}) copy-start(bf16[8,64,16,64]{3,2,1,0:T(8,128)(2,1)} %reshape.283) | copy-start | bytes 3145732
  211.2 4.4 %slice-start = ((f32[128,128]{1,0:T(8,128)}), f32[16,128]{1,0:T(8,128)S(1)}, s32[]{:S(2)}) async-start(f32[128,128]{1,0:T(8,128)} %copy-done.11), calls=%async_computation.3 | async-start | bytes 16384 | tf_op jit(solution)/shard_map/slice | solution.py:29
  211.2 4.4 %slice-start.1 = ((f32[128,128]{1,0:T(8,128)}), f32[16,128]{1,0:T(8,128)S(1)}, s32[]{:S(2)}) async-start(f32[128,128]{1,0:T(8,128)} %copy-done.12), calls=%async_computation.4 | async-start | bytes 16384 | tf_op jit(solution)/shard_map/slice | solution.py:29
  232.6 1.2 copy-start.10
  233.0 5.1 %copy-start.1 = (bf16[1024,1024]{1,0:T(8,128)(2,1)S(1)}, bf16[1024,1024]{1,0:T(8,128)(2,1)}, u32[]{:S(2)}) copy-start(bf16[1024,1024]{1,0:T(8,128)(2,1)} %param.13) | copy-start | bytes 6291460
Sparse Core Ops, SparseCore 0:
  12.6 32.9 all-gather.6
  135.0 37.2 all-gather.8
